TPU v7x, 32 devices: a whole 2x2x4 slice. The times are simulated.
32 devices in a mesh: gx: 4 (over y, x), gy: 8 (over z, core).
Axes of the slice: x: 2, y: 2, z: 4, core: 2. Of those that a mesh axis runs over, the one named last changes fastest.
Arguments:
- conserved: float32 [5, 4, 4, 4, 16, 16, 128], P(None, None, None, None, 'gx', 'gy'), as said below
- troubled_list: int32 [16384], P(('gx', 'gy')), may hold values from 0 to 1024, as said below
- widths_x: float32 [16], replicated, may hold values from 1 to 3
- widths_y: float32 [16], replicated, may hold values from 1 to 3
- widths_z: float32 [128], replicated, may hold values from 1 to 3
- speed_x: float32 [16], replicated, may hold values from -0.5 to 0.5
- speed_y: float32 [16], replicated, may hold values from -0.5 to 0.5
- speed_z: float32 [128], replicated, may hold values from -0.5 to 0.5
Outputs:
- advanced: float32 [5, 4, 4, 4, 16, 16, 128], P(None, None, None, None, 'gx', 'gy')
- hessian: float32 [6, 16, 16, 128], P(None, 'gx', 'gy')
Inputs may be any that keep to these rules, and one draw needn't show every extreme that they name: `conserved`: density lies between 0.5 and 2 and the pressure computed from the state between 0.5 and 2 at every node. `troubled_list`: in each device's block the first c entries are distinct element indices in increasing order and the rest equal 1024; c is at most 512 and reaches 512 on some device, and the c of all devices sum to exactly 8192.
All inputs are finite; a program needn't handle non-finite values.
Results may differ from a plain program's by a relative error of at most 0.0003.
Values sent between devices are 32-bit elements; how exact they have to be, the bound alone decides.
A program may use at most 64 MiB of HBM per device.

v0:
```python
import functools

import jax
import jax.numpy as jnp
import numpy as np
from jax import lax
from jax.experimental import pallas as pl
from jax.experimental.pallas import tpu as pltpu
from jax.sharding import PartitionSpec as P

MESH = pl.DeviceIdType.MESH
time_step = 0.05
gamma_ratio = 1.4


def lgl_tables():
    nodes = np.array([-1.0, -1.0 / np.sqrt(5.0), 1.0 / np.sqrt(5.0), 1.0])
    weights = np.array([1.0 / 6.0, 5.0 / 6.0, 5.0 / 6.0, 1.0 / 6.0])
    barycentric = np.ones(4)
    for row_a in range(4):
        for row_b in range(4):
            if row_a != row_b:
                barycentric[row_a] = barycentric[row_a] / (nodes[row_a] - nodes[row_b])
    deriv = np.zeros((4, 4))
    for row_a in range(4):
        for row_b in range(4):
            if row_a != row_b:
                deriv[row_a, row_b] = (
                    barycentric[row_b] / barycentric[row_a] / (nodes[row_a] - nodes[row_b])
                )
    for row_a in range(4):
        deriv[row_a, row_a] = -np.sum(deriv[row_a])
    return (nodes, weights, deriv)


NODES, WEIGHTS, DERIV = lgl_tables()
SPEED, INTER, SCALE, FACE = 0, 12, 21, 27
RATIO, MASK, GEO = 33, 34, 35


def primitives(state):
    inverse = 1.0 / state[0]
    square = state[1] * state[1] + state[2] * state[2] + state[3] * state[3]
    pressure = (gamma_ratio - 1.0) * (state[4] - 0.5 * square * inverse)
    ratio = gamma_ratio * pressure * inverse
    return inverse, pressure, ratio * lax.rsqrt(ratio)


def twice_flux(low, p_low, c_low, u_low, high, p_high, c_high, u_high, direction, speed):
    rel_low = u_low - speed
    rel_high = u_high - speed
    fastest = jnp.maximum(jnp.abs(rel_low) + c_low, jnp.abs(rel_high) + c_high)
    left = rel_low + fastest
    right = rel_high - fastest
    flux = [low[v] * left + high[v] * right for v in range(5)]
    flux[direction + 1] = flux[direction + 1] + (p_low + p_high)
    flux[4] = flux[4] + (p_low * u_low + p_high * u_high)
    return flux


def dg_apply(values):
    lifted = DERIV.copy()
    lifted[0, 0] += 1.0 / WEIGHTS[0]
    lifted[3, 3] -= 1.0 / WEIGHTS[3]
    lifted = 2.0 * WEIGHTS[:, None] * lifted
    odd_0, odd_1 = values[0] - values[3], values[1] - values[2]
    even_0, even_1 = values[0] + values[3], values[1] + values[2]
    out = [None] * 4
    for row in (0, 1):
        total = 0.5 * (lifted[row, 0] - lifted[row, 3]) * odd_0
        total = total + 0.5 * (lifted[row, 1] - lifted[row, 2]) * odd_1
        apart = 0.5 * (lifted[row, 0] + lifted[row, 3]) * even_0
        apart = apart + 0.5 * (lifted[row, 1] + lifted[row, 2]) * even_1
        out[row] = total + apart
        out[3 - row] = total - apart
    return out


def kernel(
    tile_x,
    tile_y,
    sizes,
    cons_hbm,
    list_ref,
    wx_ref,
    wy_ref,
    wz_ref,
    sx_ref,
    sy_ref,
    sz_ref,
    adv_hbm,
    hess_ref,
    state,
    out,
    inv_s,
    pres_s,
    sound_s,
    geo,
    xs,
    xr,
    ys,
    yr,
    rxs,
    rxr,
    rys,
    ryr,
    rds,
    rdr,
    io_sem,
    send_sem,
    recv_sem,
):
    size_x, size_y = sizes
    rows = tile_x * tile_y
    lanes = state.shape[-1]
    me_x, me_y = lax.axis_index("gx"), lax.axis_index("gy")
    up_x, down_x = lax.rem(me_x + 1, size_x), lax.rem(me_x + size_x - 1, size_x)
    up_y, down_y = lax.rem(me_y + 1, size_y), lax.rem(me_y + size_y - 1, size_y)

    load = pltpu.make_async_copy(cons_hbm, state, io_sem.at[0])
    load.start()
    barrier = pltpu.get_barrier_semaphore()
    partners = (
        (up_x, me_y),
        (down_x, me_y),
        (me_x, up_y),
        (me_x, down_y),
        (up_x, up_y),
        (down_x, down_y),
    )
    for partner in partners:
        pl.semaphore_signal(barrier, inc=1, device_id=partner, device_id_type=MESH)

    shape = (rows, lanes)
    row = lax.broadcasted_iota(jnp.int32, shape, 0)
    row_i, row_j = row // tile_y, row % tile_y

    def roll_rows(value, shift):
        shift = shift % rows
        return value if shift == 0 else pltpu.roll(value, shift, 0)

    def roll_lanes(value, shift):
        return pltpu.roll(value, shift % lanes, 1)

    def along(ref, start, total, tile, index):
        values = [ref[lax.rem(start + total + i, total)] for i in range(-1, tile + 1)]

        def pick(offset):
            vector = jnp.full(shape, values[1 + offset], jnp.float32)
            for i in range(1, tile):
                vector = jnp.where(index == i, values[1 + offset + i], vector)
            return vector

        return pick(-1), pick(0), pick(1)

    total_x, total_y = size_x * tile_x, size_y * tile_y
    wx_p, wx, _ = along(wx_ref, me_x * tile_x, total_x, tile_x, row_i)
    wy_p, wy, _ = along(wy_ref, me_y * tile_y, total_y, tile_y, row_j)
    sx_p, sx, sx_n = along(sx_ref, me_x * tile_x, total_x, tile_x, row_i)
    sy_p, sy, sy_n = along(sy_ref, me_y * tile_y, total_y, tile_y, row_j)
    wz = jnp.broadcast_to(wz_ref[...], shape)
    sz = jnp.broadcast_to(sz_ref[...], shape)
    sz_n = roll_lanes(sz, -1)
    nx, ny, nz = (
        wx + time_step * (sx_n - sx),
        wy + time_step * (sy_n - sy),
        wz + time_step * (sz_n - sz),
    )
    px, py = wx_p + time_step * (sx - sx_p), wy_p + time_step * (sy - sy_p)
    pz = roll_lanes(nz, 1)
    mass = nx * ny * nz
    ratio = wx * wy * wz / mass
    geo[RATIO] = ratio
    for d, (width, low, high) in enumerate(((wx, sx, sx_n), (wy, sy, sy_n), (wz, sz, sz_n))):
        for a in range(4):
            geo[SPEED + 4 * d + a] = low * float((1.0 - NODES[a]) / 2.0) + high * float(
                (1.0 + NODES[a]) / 2.0
            )
        for q, xi in enumerate((-5.0 / 6.0, 0.0, 5.0 / 6.0)):
            geo[INTER + 3 * d + q] = low * ((1.0 - xi) / 2.0) + high * ((1.0 + xi) / 2.0)
        geo[FACE + 2 * d] = low
        geo[FACE + 2 * d + 1] = high
        kappa = -time_step * ratio / width
        geo[SCALE + 2 * d] = kappa * float(1.0 / WEIGHTS[0])
        geo[SCALE + 2 * d + 1] = kappa * float(1.0 / WEIGHTS[1])

    entries = list_ref[...]
    count = entries.shape[-1]
    in_row = jnp.where(
        lax.broadcasted_iota(jnp.int32, (rows, count), 0) == entries // lanes, 1.0, 0.0
    )
    in_lane = jnp.where(
        lax.broadcasted_iota(jnp.int32, (lanes, count), 0) == entries % lanes, 1.0, 0.0
    )
    geo[MASK] = lax.dot_general(
        in_row, in_lane, (((1,), (1,)), ((), ())), preferred_element_type=jnp.float32
    )

    load.wait()

    def pack_faces(q, carry):
        for v in range(5):
            for side, node, first in ((0, 0, 0), (1, 3, rows - tile_y)):
                packed = None
                for c in range(4):
                    part = roll_rows(state[v, node, q, c], tile_y * c - first)
                    packed = part if packed is None else jnp.where(row_i == c, part, packed)
                xs[side, v, q] = packed
            for side, node, first in ((0, 0, 0), (1, 3, tile_y - 1)):
                for group in range(4 // tile_y):
                    packed = None
                    for c in range(tile_y):
                        part = roll_rows(state[v, q, node, group * tile_y + c], c - first)
                        packed = part if packed is None else jnp.where(row_j == c, part, packed)
                    ys[side, v, q, group] = packed
        return carry

    lax.fori_loop(0, 4, pack_faces, 0)
    pl.semaphore_wait(barrier, len(partners))

    def remote(src, dst, slot, device):
        return pltpu.make_async_remote_copy(
            src_ref=src,
            dst_ref=dst,
            send_sem=send_sem.at[slot],
            recv_sem=recv_sem.at[slot],
            device_id=device,
            device_id_type=MESH,
        )

    faces = [
        remote(ys.at[0], yr.at[1], 2, (me_x, down_y)),
        remote(ys.at[1], yr.at[0], 3, (me_x, up_y)),
        remote(xs.at[0], xr.at[1], 0, (down_x, me_y)),
        remote(xs.at[1], xr.at[0], 1, (up_x, me_y)),
    ]
    for copy in faces:
        copy.start()

    def prepare(index, carry):
        a, b = index // 4, index % 4
        for c in range(4):
            inverse, pressure, sound = primitives([state[v, a, b, c] for v in range(5)])
            inv_s[a, b, c] = inverse
            pres_s[a, b, c] = pressure
            sound_s[a, b, c] = sound
        return carry

    lax.fori_loop(0, 16, prepare, 0)

    def interior(d, index, carry):
        first, second = index // 4, index % 4

        def at(n):
            return ((n, first, second), (first, n, second), (first, second, n))[d]

        mask = geo[MASK] > 0.5
        states = [[state[(v,) + at(n)] for v in range(5)] for n in range(4)]
        pressure = [pres_s[at(n)] for n in range(4)]
        sound = [sound_s[at(n)] for n in range(4)]
        normal = [states[n][d + 1] * inv_s[at(n)] for n in range(4)]
        inner = [
            twice_flux(
                states[q],
                pressure[q],
                sound[q],
                normal[q],
                states[q + 1],
                pressure[q + 1],
                sound[q + 1],
                normal[q + 1],
                d,
                geo[INTER + 3 * d + q],
            )
            for q in range(3)
        ]
        relative = [normal[n] - geo[SPEED + 4 * d + n] for n in range(4)]
        if d == 2:
            star_low = twice_flux(
                [roll_lanes(states[3][v], 1) for v in range(5)],
                roll_lanes(pressure[3], 1),
                roll_lanes(sound[3], 1),
                roll_lanes(normal[3], 1),
                states[0],
                pressure[0],
                sound[0],
                normal[0],
                d,
                geo[FACE + 2 * d],
            )
        for v in range(5):
            flux = [states[n][v] * relative[n] for n in range(4)]
            if v == d + 1:
                flux = [flux[n] + pressure[n] for n in range(4)]
            if v == 4:
                flux = [flux[n] + pressure[n] * normal[n] for n in range(4)]
            smooth = dg_apply(flux)
            fv = [inner[0][v], inner[1][v] - inner[0][v], inner[2][v] - inner[1][v], -inner[2][v]]
            chosen = [jnp.where(mask, fv[n], smooth[n]) for n in range(4)]
            if d == 2:
                chosen[0] = chosen[0] - star_low[v]
                chosen[3] = chosen[3] + roll_lanes(star_low[v], -1)
            for n in range(4):
                where = (v,) + at(n)
                scale = geo[SCALE + 2 * d + (0 if n in (0, 3) else 1)]
                if d == 0:
                    base = geo[RATIO] * states[n][v]
                else:
                    base = out[where]
                out[where] = base + scale * chosen[n]
        return carry

    for d in range(3):
        lax.fori_loop(0, 16, functools.partial(interior, d), 0)

    def surface(d, q, carry):
        for c in range(4):
            at = ((lambda n: (n, q, c)), (lambda n: (q, n, c)))[d]
            scale = geo[SCALE + 2 * d]
            shift = (tile_y, 1)[d]
            edge = (row_i, row_j)[d]
            last = (tile_x, tile_y)[d] - 1
            for side, node, far in ((0, 0, 3), (1, 3, 0)):
                own = [state[(v,) + at(node)] for v in range(5)]
                other = []
                for v in range(5):
                    if d == 0:
                        to = 0 if side == 0 else rows - tile_y
                        halo = roll_rows(xr[side, v, q], to - tile_y * c)
                    else:
                        to = 0 if side == 0 else tile_y - 1
                        halo = roll_rows(yr[side, v, q, c // tile_y], to - c % tile_y)
                    moved = roll_rows(state[(v,) + at(far)], shift if side == 0 else -shift)
                    other.append(jnp.where(edge == (0 if side == 0 else last), halo, moved))
                inverse, pressure, sound = primitives(other)
                own_side = (
                    own,
                    pres_s[at(node)],
                    sound_s[at(node)],
                    own[d + 1] * inv_s[at(node)],
                )
                other_side = (other, pressure, sound, other[d + 1] * inverse)
                low, high = (other_side, own_side) if side == 0 else (own_side, other_side)
                star = twice_flux(*low, *high, d, geo[FACE + 2 * d + side])
                for v in range(5):
                    where = (v,) + at(node)
                    if side == 0:
                        out[where] = out[where] - scale * star[v]
                    else:
                        out[where] = out[where] + scale * star[v]
        return carry

    faces[2].wait()
    faces[3].wait()
    lax.fori_loop(0, 4, functools.partial(surface, 0), 0)
    faces[0].wait()
    faces[1].wait()
    lax.fori_loop(0, 4, functools.partial(surface, 1), 0)

    store = pltpu.make_async_copy(out, adv_hbm, io_sem.at[1])
    store.start()

    second = DERIV @ DERIV
    ends = (0, 3)

    def combine(coefficients, values):
        total = float(coefficients[0]) * values[0]
        for n in range(1, 4):
            total = total + float(coefficients[n]) * values[n]
        return total

    density = [[[out[0, a, b, c] for c in range(4)] for b in range(4)] for a in range(4)]
    ix, iy, iz = 2.0 / nx, 2.0 / ny, 2.0 / nz
    factors = (
        mass * ix * ix,
        mass * iy * iy,
        mass * iz * iz,
        mass * ix * iy,
        mass * ix * iz,
        mass * iy * iz,
    )
    along_x = {
        (p, b, c): combine(DERIV[p], [density[a][b][c] for a in range(4)])
        for p in ends
        for b in range(4)
        for c in range(4)
        if b in ends or c in ends
    }
    along_y = {
        (a, q, c): combine(DERIV[q], [density[a][b][c] for b in range(4)])
        for q in ends
        for a in ends
        for c in range(4)
    }

    def corner(kind, p, q, r):
        if kind == 0:
            return combine(second[p], [density[a][q][r] for a in range(4)])
        if kind == 1:
            return combine(second[q], [density[p][b][r] for b in range(4)])
        if kind == 2:
            return combine(second[r], [density[p][q][c] for c in range(4)])
        if kind == 3:
            return combine(DERIV[q], [along_x[p, b, r] for b in range(4)])
        if kind == 4:
            return combine(DERIV[r], [along_x[p, q, c] for c in range(4)])
        return combine(DERIV[r], [along_y[p, q, c] for c in range(4)])

    own_sum = []
    x_rim = [None] * -(-6 // tile_x)
    y_rim = [None] * -(-6 // tile_y)
    d_rim = None
    for kind in range(6):
        column = {}
        for p in ends:
            for q in ends:
                low = factors[kind] * corner(kind, p, q, 0)
                high = factors[kind] * corner(kind, p, q, 3)
                column[p, q] = low + roll_lanes(high, 1)
        def up_y_shift(value):
            return jnp.where(row_j == 0, 0.0, roll_rows(value, 1))

        low_x = column[0, 0] + up_y_shift(column[0, 3])
        high_x = column[3, 0] + up_y_shift(column[3, 3])
        moved = jnp.where(row_i == 0, 0.0, roll_rows(high_x, tile_y))
        own_sum.append(low_x + moved)
        slot, place = kind // tile_x, kind % tile_x
        part = roll_rows(high_x, tile_y * place - (rows - tile_y))
        x_rim[slot] = part if place == 0 else jnp.where(row_i == place, part, x_rim[slot])
        rim = column[0, 3] + jnp.where(row_i == 0, 0.0, roll_rows(column[3, 3], tile_y))
        slot, place = kind // tile_y, kind % tile_y
        part = roll_rows(rim, place - (tile_y - 1))
        y_rim[slot] = part if place == 0 else jnp.where(row_j == place, part, y_rim[slot])
        part = roll_rows(column[3, 3], kind - (rows - 1))
        d_rim = part if kind == 0 else jnp.where(row == kind, part, d_rim)
    for slot, value in enumerate(x_rim):
        rxs[slot] = value
    for slot, value in enumerate(y_rim):
        rys[slot] = value
    rds[...] = d_rim
    rims = [
        remote(rds, rdr, 6, (up_x, up_y)),
        remote(rys, ryr, 5, (me_x, up_y)),
        remote(rxs, rxr, 4, (up_x, me_y)),
    ]
    for copy in rims:
        copy.start()
    inverse = 1.0 / ((nx + px) * (ny + py) * (nz + pz))
    for kind in range(6):
        hess_ref[kind] = own_sum[kind]
    for copy in rims:
        copy.wait()
    for kind in range(6):
        total = hess_ref[kind]
        from_x = roll_rows(rxr[kind // tile_x], -tile_y * (kind % tile_x))
        total = total + jnp.where(row_i == 0, from_x, 0.0)
        from_y = roll_rows(ryr[kind // tile_y], -(kind % tile_y))
        total = total + jnp.where(row_j == 0, from_y, 0.0)
        total = total + jnp.where(row == 0, roll_rows(rdr[...], -kind), 0.0)
        hess_ref[kind] = total * inverse
    store.wait()


def solution(mesh):
    sizes = (mesh.shape["gx"], mesh.shape["gy"])

    def local(conserved, troubled_list, widths_x, widths_y, widths_z, speed_x, speed_y, speed_z):
        tile_x, tile_y, column = conserved.shape[4:]
        rows = tile_x * tile_y
        f32 = jnp.float32
        smem = pl.BlockSpec(memory_space=pltpu.SMEM)
        vmem = pl.BlockSpec(memory_space=pltpu.VMEM)
        whole = pl.BlockSpec(memory_space=pl.ANY)
        full = (5, 4, 4, 4, rows, column)
        nodal = (4, 4, 4, rows, column)
        x_face = (2, 5, 4, rows, column)
        y_face = (2, 5, 4, 4 // tile_y, rows, column)
        x_rim = (-(-6 // tile_x), rows, column)
        y_rim = (-(-6 // tile_y), rows, column)
        advanced, hessian = pl.pallas_call(
            functools.partial(kernel, tile_x, tile_y, sizes),
            out_shape=(
                jax.ShapeDtypeStruct(full, f32),
                jax.ShapeDtypeStruct((6, rows, column), f32),
            ),
            in_specs=[whole, vmem, smem, smem, vmem, smem, smem, vmem],
            out_specs=(whole, vmem),
            scratch_shapes=[
                pltpu.VMEM(full, f32),
                pltpu.VMEM(full, f32),
                pltpu.VMEM(nodal, f32),
                pltpu.VMEM(nodal, f32),
                pltpu.VMEM(nodal, f32),
                pltpu.VMEM((GEO, rows, column), f32),
                pltpu.VMEM(x_face, f32),
                pltpu.VMEM(x_face, f32),
                pltpu.VMEM(y_face, f32),
                pltpu.VMEM(y_face, f32),
                pltpu.VMEM(x_rim, f32),
                pltpu.VMEM(x_rim, f32),
                pltpu.VMEM(y_rim, f32),
                pltpu.VMEM(y_rim, f32),
                pltpu.VMEM((rows, column), f32),
                pltpu.VMEM((rows, column), f32),
                pltpu.SemaphoreType.DMA((2,)),
                pltpu.SemaphoreType.DMA((7,)),
                pltpu.SemaphoreType.DMA((7,)),
            ],
            compiler_params=pltpu.CompilerParams(collective_id=0, has_side_effects=True),
        )(
            conserved.reshape(full),
            troubled_list.reshape(1, -1),
            widths_x,
            widths_y,
            widths_z.reshape(1, -1),
            speed_x,
            speed_y,
            speed_z.reshape(1, -1),
        )
        return advanced.reshape(conserved.shape), hessian.reshape(6, tile_x, tile_y, column)

    in_specs = (
        P(None, None, None, None, "gx", "gy", None),
        P(("gx", "gy")),
        P(),
        P(),
        P(),
        P(),
        P(),
        P(),
    )
    out_specs = (P(None, None, None, None, "gx", "gy", None), P(None, "gx", "gy", None))
    return jax.shard_map(local, mesh=mesh, in_specs=in_specs, out_specs=out_specs, check_vma=False)
```

profile of v0, /device:TPU:0, one launch (start us, length us, event | category | flops | bytes accessed | tf_op | source)
XLA Modules:
  0.0 20.8 jit_solution(874423893089542215)
XLA Ops:
  0.6 16.5 %shard_map.95 = (f32[5,4,4,4,8,128]{5,4,3,2,1,0:T(8,128)}, f32[6,8,128]{2,1,0:T(8,128)}) custom-call(f32[5,4,4,4,8,128]{5,4,3,2,1,0:T(8,128)} %bitcast.6, s32[1,512]{1,0:T(1,128)} %bitcast.9, f32[16]{0:T(128)} %wx_ref.1, f32[16]{0:T(128)} %wy_ref.1, f32[1,128]{1,0:T(1,128)} %bitcast.10, f32[16]{0:T(128)} %sx_ref.1, f32[16]{0:T(128)} %sy_ref.1, f32[1,128]{1,0:T(1,128)} %bitcast.11), custom_call_target="tpu_custom_call" | custom-call | tf_op jit(solution)/shard_map/pallas_call | solution.py:480
  17.2 0.0 copy-start
  17.2 3.0 %copy.12 = f32[5,4,4,4,4,2,128]{6,5,4,3,2,1,0:T(2,128)} copy(f32[5,4,4,4,4,2,128]{6,5,4,3,2,1,0:T(2,128)} %bitcast.7) | data formatting | bytes 2621440
  20.2 0.0 copy-done
  20.2 0.6 %copy.13 = f32[6,4,2,128]{3,2,1,0:T(2,128)} copy(f32[6,4,2,128]{3,2,1,0:T(2,128)S(1)} %bitcast.8) | data formatting | bytes 49152
Async XLA Ops:
  17.2 3.0 %copy-start = (f32[6,8,128]{2,1,0:T(8,128)S(1)}, f32[6,8,128]{2,1,0:T(8,128)}, u32[]{:S(2)}) copy-start(f32[6,8,128]{2,1,0:T(8,128)} %get-tuple-element.5) | copy-start | bytes 73732
where the time goes:
time: 21 us; the launch traced here: 20.8 us
  Pallas kernels  16.5 us (79%)
  local copies, waits for them, and re-layouts  3.64 us (17%)
  between operations  0.65 us (3%)
    pallas_call x1, Pallas kernels, local(): pl.pallas_call(functools.partial(kernel, tile_x, tile_y, sizes), out_shap...  16.5 us
    unnamed x4, local copies, waits for them, and re-layouts  3.64 us

commit v1 on v0

--- a/solution.py
+++ b/solution.py
@@ -36,6 +36,9 @@
 NODES, WEIGHTS, DERIV = lgl_tables()
 SPEED, INTER, SCALE, FACE = 0, 12, 21, 27
 RATIO, MASK, GEO = 33, 34, 35
+ALL, DENSITY, REST = (0, 1, 2, 3, 4), (0,), (1, 2, 3, 4)
+FIRST = ((0, ALL), (1, ALL), (2, DENSITY))
+LATER = ((2, REST),)
 
 
 def primitives(state):
@@ -81,6 +84,15 @@
     tile_y,
     sizes,
     cons_hbm,
+    list_hbm,
+    wx_hbm,
+    wy_hbm,
+    wz_hbm,
+    sx_hbm,
+    sy_hbm,
+    sz_hbm,
+    out,
+    hess_ref,
     list_ref,
     wx_ref,
     wy_ref,
@@ -88,10 +100,7 @@
     sx_ref,
     sy_ref,
     sz_ref,
-    adv_hbm,
-    hess_ref,
     state,
-    out,
     inv_s,
     pres_s,
     sound_s,
@@ -117,19 +126,29 @@
     up_x, down_x = lax.rem(me_x + 1, size_x), lax.rem(me_x + size_x - 1, size_x)
     up_y, down_y = lax.rem(me_y + 1, size_y), lax.rem(me_y + size_y - 1, size_y)
 
-    load = pltpu.make_async_copy(cons_hbm, state, io_sem.at[0])
-    load.start()
     barrier = pltpu.get_barrier_semaphore()
-    partners = (
-        (up_x, me_y),
-        (down_x, me_y),
-        (me_x, up_y),
-        (me_x, down_y),
-        (up_x, up_y),
-        (down_x, down_y),
-    )
+    partners = ((me_x, down_y), (me_x, up_y), (down_x, me_y), (up_x, me_y))
     for partner in partners:
         pl.semaphore_signal(barrier, inc=1, device_id=partner, device_id_type=MESH)
+    small = [
+        pltpu.make_async_copy(src, dst, io_sem.at[4 + n])
+        for n, (src, dst) in enumerate(
+            (
+                (wx_hbm, wx_ref),
+                (wy_hbm, wy_ref),
+                (sx_hbm, sx_ref),
+                (sy_hbm, sy_ref),
+                (wz_hbm, wz_ref),
+                (sz_hbm, sz_ref),
+                (list_hbm, list_ref),
+            )
+        )
+    ]
+    loads = [pltpu.make_async_copy(cons_hbm.at[:, a], state.at[:, a], io_sem.at[a]) for a in range(4)]
+    for a in (0, 3, 1, 2):
+        loads[a].start()
+    for copy in small:
+        copy.start()
 
     shape = (rows, lanes)
     row = lax.broadcasted_iota(jnp.int32, shape, 0)
@@ -141,6 +160,56 @@
 
     def roll_lanes(value, shift):
         return pltpu.roll(value, shift % lanes, 1)
+
+    def pack_x(q, carry):
+        for v in range(5):
+            for side, node, first in ((0, 0, 0), (1, 3, rows - tile_y)):
+                packed = None
+                for c in range(4):
+                    part = roll_rows(state[v, node, q, c], tile_y * c - first)
+                    packed = part if packed is None else jnp.where(row_i == c, part, packed)
+                xs[side, v, q] = packed
+        return carry
+
+    def pack_y(q, carry):
+        for v in range(5):
+            for side, node, first in ((0, 0, 0), (1, 3, tile_y - 1)):
+                for group in range(4 // tile_y):
+                    packed = None
+                    for c in range(tile_y):
+                        part = roll_rows(state[v, q, node, group * tile_y + c], c - first)
+                        packed = part if packed is None else jnp.where(row_j == c, part, packed)
+                    ys[side, v, q, group] = packed
+        return carry
+
+    for a in (0, 3, 1, 2):
+        loads[a].wait()
+        pack_y(a, 0)
+    pl.semaphore_wait(barrier, len(partners))
+
+    def remote(src, dst, slot, device):
+        return pltpu.make_async_remote_copy(
+            src_ref=src,
+            dst_ref=dst,
+            send_sem=send_sem.at[slot],
+            recv_sem=recv_sem.at[slot],
+            device_id=device,
+            device_id_type=MESH,
+        )
+
+    faces = [
+        remote(ys.at[0], yr.at[1], 2, (me_x, down_y)),
+        remote(ys.at[1], yr.at[0], 3, (me_x, up_y)),
+        remote(xs.at[0], xr.at[1], 0, (down_x, me_y)),
+        remote(xs.at[1], xr.at[0], 1, (up_x, me_y)),
+    ]
+    faces[0].start()
+    faces[1].start()
+    lax.fori_loop(0, 4, pack_x, 0)
+    faces[2].start()
+    faces[3].start()
+    for copy in small:
+        copy.wait()
 
     def along(ref, start, total, tile, index):
         values = [ref[lax.rem(start + total + i, total)] for i in range(-1, tile + 1)]
@@ -196,47 +265,6 @@
         in_row, in_lane, (((1,), (1,)), ((), ())), preferred_element_type=jnp.float32
     )
 
-    load.wait()
-
-    def pack_faces(q, carry):
-        for v in range(5):
-            for side, node, first in ((0, 0, 0), (1, 3, rows - tile_y)):
-                packed = None
-                for c in range(4):
-                    part = roll_rows(state[v, node, q, c], tile_y * c - first)
-                    packed = part if packed is None else jnp.where(row_i == c, part, packed)
-                xs[side, v, q] = packed
-            for side, node, first in ((0, 0, 0), (1, 3, tile_y - 1)):
-                for group in range(4 // tile_y):
-                    packed = None
-                    for c in range(tile_y):
-                        part = roll_rows(state[v, q, node, group * tile_y + c], c - first)
-                        packed = part if packed is None else jnp.where(row_j == c, part, packed)
-                    ys[side, v, q, group] = packed
-        return carry
-
-    lax.fori_loop(0, 4, pack_faces, 0)
-    pl.semaphore_wait(barrier, len(partners))
-
-    def remote(src, dst, slot, device):
-        return pltpu.make_async_remote_copy(
-            src_ref=src,
-            dst_ref=dst,
-            send_sem=send_sem.at[slot],
-            recv_sem=recv_sem.at[slot],
-            device_id=device,
-            device_id_type=MESH,
-        )
-
-    faces = [
-        remote(ys.at[0], yr.at[1], 2, (me_x, down_y)),
-        remote(ys.at[1], yr.at[0], 3, (me_x, up_y)),
-        remote(xs.at[0], xr.at[1], 0, (down_x, me_y)),
-        remote(xs.at[1], xr.at[0], 1, (up_x, me_y)),
-    ]
-    for copy in faces:
-        copy.start()
-
     def prepare(index, carry):
         a, b = index // 4, index % 4
         for c in range(4):
@@ -248,7 +276,7 @@
 
     lax.fori_loop(0, 16, prepare, 0)
 
-    def interior(d, index, carry):
+    def interior(d, parts, index, carry):
         first, second = index // 4, index % 4
 
         def at(n):
@@ -288,7 +316,7 @@
                 d,
                 geo[FACE + 2 * d],
             )
-        for v in range(5):
+        for v in parts:
             flux = [states[n][v] * relative[n] for n in range(4)]
             if v == d + 1:
                 flux = [flux[n] + pressure[n] for n in range(4)]
@@ -310,10 +338,10 @@
                 out[where] = base + scale * chosen[n]
         return carry
 
-    for d in range(3):
-        lax.fori_loop(0, 16, functools.partial(interior, d), 0)
-
-    def surface(d, q, carry):
+    for d, parts in FIRST:
+        lax.fori_loop(0, 16, functools.partial(interior, d, parts), 0)
+
+    def surface(d, parts, q, carry):
         for c in range(4):
             at = ((lambda n: (n, q, c)), (lambda n: (q, n, c)))[d]
             scale = geo[SCALE + 2 * d]
@@ -342,7 +370,7 @@
                 other_side = (other, pressure, sound, other[d + 1] * inverse)
                 low, high = (other_side, own_side) if side == 0 else (own_side, other_side)
                 star = twice_flux(*low, *high, d, geo[FACE + 2 * d + side])
-                for v in range(5):
+                for v in parts:
                     where = (v,) + at(node)
                     if side == 0:
                         out[where] = out[where] - scale * star[v]
@@ -352,13 +380,10 @@
 
     faces[2].wait()
     faces[3].wait()
-    lax.fori_loop(0, 4, functools.partial(surface, 0), 0)
+    lax.fori_loop(0, 4, functools.partial(surface, 0, (0,)), 0)
     faces[0].wait()
     faces[1].wait()
-    lax.fori_loop(0, 4, functools.partial(surface, 1), 0)
-
-    store = pltpu.make_async_copy(out, adv_hbm, io_sem.at[1])
-    store.start()
+    lax.fori_loop(0, 4, functools.partial(surface, 1, (0,)), 0)
 
     second = DERIV @ DERIV
     ends = (0, 3)
@@ -445,6 +470,10 @@
     ]
     for copy in rims:
         copy.start()
+    for d, parts in LATER:
+        lax.fori_loop(0, 16, functools.partial(interior, d, parts), 0)
+    for d in range(2):
+        lax.fori_loop(0, 4, functools.partial(surface, d, (1, 2, 3, 4)), 0)
     inverse = 1.0 / ((nx + px) * (ny + py) * (nz + pz))
     for kind in range(6):
         hess_ref[kind] = own_sum[kind]
@@ -458,7 +487,17 @@
         total = total + jnp.where(row_j == 0, from_y, 0.0)
         total = total + jnp.where(row == 0, roll_rows(rdr[...], -kind), 0.0)
         hess_ref[kind] = total * inverse
-    store.wait()
+
+
+def emit(adv_ref, hess_ref, adv_out, hess_out, sem):
+    copies = [
+        pltpu.make_async_copy(adv_ref, adv_out, sem.at[0]),
+        pltpu.make_async_copy(hess_ref, hess_out, sem.at[1]),
+    ]
+    for copy in copies:
+        copy.start()
+    for copy in copies:
+        copy.wait()
 
 
 def solution(mesh):
@@ -468,7 +507,6 @@
         tile_x, tile_y, column = conserved.shape[4:]
         rows = tile_x * tile_y
         f32 = jnp.float32
-        smem = pl.BlockSpec(memory_space=pltpu.SMEM)
         vmem = pl.BlockSpec(memory_space=pltpu.VMEM)
         whole = pl.BlockSpec(memory_space=pl.ANY)
         full = (5, 4, 4, 4, rows, column)
@@ -480,13 +518,19 @@
         advanced, hessian = pl.pallas_call(
             functools.partial(kernel, tile_x, tile_y, sizes),
             out_shape=(
-                jax.ShapeDtypeStruct(full, f32),
-                jax.ShapeDtypeStruct((6, rows, column), f32),
+                pltpu.VMEM(full, f32),
+                pltpu.VMEM((6, rows, column), f32),
             ),
-            in_specs=[whole, vmem, smem, smem, vmem, smem, smem, vmem],
-            out_specs=(whole, vmem),
+            in_specs=[whole] * 8,
+            out_specs=(vmem, vmem),
             scratch_shapes=[
-                pltpu.VMEM(full, f32),
+                pltpu.VMEM((1, troubled_list.shape[0]), jnp.int32),
+                pltpu.SMEM(widths_x.shape, f32),
+                pltpu.SMEM(widths_y.shape, f32),
+                pltpu.VMEM((1, column), f32),
+                pltpu.SMEM(speed_x.shape, f32),
+                pltpu.SMEM(speed_y.shape, f32),
+                pltpu.VMEM((1, column), f32),
                 pltpu.VMEM(full, f32),
                 pltpu.VMEM(nodal, f32),
                 pltpu.VMEM(nodal, f32),
@@ -502,7 +546,7 @@
                 pltpu.VMEM(y_rim, f32),
                 pltpu.VMEM((rows, column), f32),
                 pltpu.VMEM((rows, column), f32),
-                pltpu.SemaphoreType.DMA((2,)),
+                pltpu.SemaphoreType.DMA((11,)),
                 pltpu.SemaphoreType.DMA((7,)),
                 pltpu.SemaphoreType.DMA((7,)),
             ],
@@ -517,6 +561,18 @@
             speed_y,
             speed_z.reshape(1, -1),
         )
+        advanced = pltpu.with_memory_space_constraint(advanced, pltpu.VMEM)
+        hessian = pltpu.with_memory_space_constraint(hessian, pltpu.VMEM)
+        advanced, hessian = pl.pallas_call(
+            emit,
+            out_shape=(
+                jax.ShapeDtypeStruct(full, f32),
+                jax.ShapeDtypeStruct((6, rows, column), f32),
+            ),
+            in_specs=[whole, whole],
+            out_specs=(whole, whole),
+            scratch_shapes=[pltpu.SemaphoreType.DMA((2,))],
+        )(advanced, hessian)
         return advanced.reshape(conserved.shape), hessian.reshape(6, tile_x, tile_y, column)
 
     in_specs = (

time: 21 us -> 16.8 us (0.80)
  local copies, waits for them, and re-layouts: 3.64 us -> 0 us
  Pallas kernels: 16.5 us -> 16 us
    unnamed x4 -> x0, local copies, waits for them, and re-layouts: 3.64 us -> none
    pallas_call x1, Pallas kernels: 16.5 us -> 14.9 us  [local(): pl.pallas_call(functools.partial(kernel, tile_x, tile_y, sizes), out_shap...]
    pallas_call x0 -> x1, Pallas kernels: none -> 1.08 us  [local(): pl.pallas_call(emit, out_shape=(jax.ShapeDtypeStruct(full, f32), jax.Shap...]
where the time goes in v1:
time: 16.8 us; the launch traced here: 16.6 us
  Pallas kernels  16 us (95%)
  between operations  0.64 us (4%)
    pallas_call x1, Pallas kernels, local(): pl.pallas_call(functools.partial(kernel, tile_x, tile_y, sizes), out_shap...  14.9 us
    pallas_call x1, Pallas kernels, local(): pl.pallas_call(emit, out_shape=(jax.ShapeDtypeStruct(full, f32), jax.Shap...  1.08 us

profile of v1, /device:TPU:0, one launch (start us, length us, event | category | flops | bytes accessed | tf_op | source)
XLA Modules:
  0.0 16.6 jit_solution(9457826029333169797)
XLA Ops:
  0.6 14.9 %shard_map.95 = (f32[5,4,4,4,8,128]{5,4,3,2,1,0:T(8,128)S(1)}, f32[6,8,128]{2,1,0:T(8,128)S(1)}) custom-call(f32[5,4,4,4,8,128]{5,4,3,2,1,0:T(8,128)} %bitcast.6, s32[1,512]{1,0:T(1,128)} %bitcast.7, f32[16]{0:T(128)} %wx_hbm.1, f32[16]{0:T(128)} %wy_hbm.1, f32[1,128]{1,0:T(1,128)} %bitcast.8, f32[16]{0:T(128)} %sx_hbm.1, f32[16]{0:T(128)} %sy_hbm.1, ...), custom_call_target="tpu_custom_call" | custom-call | tf_op jit(solution)/shard_map/pallas_call | solution.py:518
  15.6 1.1 %shard_map.96 = (f32[5,4,4,4,8,128]{5,4,3,2,1,0:T(8,128)}, f32[6,8,128]{2,1,0:T(8,128)}) custom-call(f32[5,4,4,4,8,128]{5,4,3,2,1,0:T(8,128)S(1)} %get-tuple-element.6.adv_ref, f32[6,8,128]{2,1,0:T(8,128)S(1)} %get-tuple-element.7.hess_ref), custom_call_target="tpu_custom_call" | custom-call | tf_op jit(solution)/shard_map/pallas_call | solution.py:566
